TPU v7x, 32 devices: a whole 2x2x4 slice. The times are simulated.
32 devices in a mesh: section: 4 (over x, core), expert: 4 (over z), tensor: 2 (over y).
Axes of the slice: x: 2, y: 2, z: 4, core: 2. Of those that a mesh axis runs over, the one named last changes fastest.
Arguments:
- tokens: bfloat16 [2048, 5120], P(('section', 'expert'), 'tensor'), may hold values from -6 to 6
- norm_gain: float32 [5120], P('tensor'), may hold values from 0.1 to 1.9
- router: bfloat16 [5120, 4], P('tensor'), may hold values from -0.078125 to 0.078125
- expert_ids: int32 [2048, 1], P(('section', 'expert')), may hold values from 0 to 3; in each aligned block of 128 rows (0 to 127, 128 to 255, ...) at most 64 rows name the same one
- gate_proj: bfloat16 [4, 5120, 4096], P('expert', None, ('section', 'tensor')), may hold values from -0.078125 to 0.078125
- up_proj: bfloat16 [4, 5120, 4096], P('expert', None, ('section', 'tensor')), may hold values from -0.078125 to 0.078125
- down_proj: bfloat16 [4, 4096, 5120], P('expert', 'section', 'tensor'), may hold values from -0.09375 to 0.09375
Outputs:
- moe_out: bfloat16 [2048, 5120], P(('section', 'expert'), 'tensor')
Inputs may be any that keep to these rules, and one draw needn't show every extreme that they name: `expert_ids`: within each aligned block of 128 tokens (the tokens of one group of devices along section and expert) no expert is named by more than 64 tokens, a bound that some block reaches.
All inputs are finite; a program needn't handle non-finite values.
Results may differ from a plain program's by a relative error of at most 0.017.
Values may be sent and summed in bfloat16 or wider, within the bound.
A program may use at most 64 MiB of HBM per device.

v0:
```python
import jax
import jax.numpy as jnp
from jax import lax
from jax.sharding import PartitionSpec as P

D = 5120


EPSILON = 1e-05


def slot_table(expert_ids, experts, capacity):
    chosen = expert_ids[:, 0]
    member = (chosen[:, None] == jnp.arange(experts, dtype=jnp.int32)[None, :]).astype(jnp.int32)
    earlier = jnp.cumsum(member, axis=0) - member
    placed = chosen * capacity + jnp.sum(earlier * member, axis=1)
    placing = placed[:, None] == jnp.arange(experts * capacity, dtype=jnp.int32)[None, :]
    return (member, placing)


def normalize(tokens, norm_gain, squares):
    values = tokens.astype(jnp.float32)
    return (values * lax.rsqrt(squares / D + EPSILON) * norm_gain).astype(jnp.bfloat16)


def on_device(tokens, norm_gain, router, expert_ids, gate_proj, up_proj, down_proj):
    row_count = tokens.shape[0]
    experts = router.shape[1]
    capacity = 2 * row_count // experts
    values = tokens.astype(jnp.float32)
    squares = lax.psum(jnp.sum(values * values, axis=1, keepdims=True), "tensor")
    normed = normalize(tokens, norm_gain, squares)
    logits = lax.psum(jnp.dot(normed, router, preferred_element_type=jnp.float32), "tensor")
    member, placing = slot_table(expert_ids, experts, capacity)
    score = jax.nn.sigmoid(jnp.sum(jnp.where(member > 0, logits, jnp.float32(0.0)), axis=1))
    routed = (normed.astype(jnp.float32) * score[:, None]).astype(jnp.bfloat16)
    placing = placing.astype(jnp.bfloat16)
    outgoing = jnp.einsum("tc,td->cd", placing, routed, preferred_element_type=jnp.float32).astype(
        jnp.bfloat16
    )
    arrived = lax.all_to_all(outgoing, "expert", split_axis=0, concat_axis=0, tiled=True)
    gate_cols = gate_proj[0]
    up_cols = up_proj[0]
    down_rows = down_proj[0]
    widened = lax.all_gather(arrived, "tensor", axis=1, tiled=True)
    piece = lax.all_gather(widened, "section", axis=0, tiled=True)
    gate = jnp.dot(piece, gate_cols, preferred_element_type=jnp.float32)
    upper = jnp.dot(piece, up_cols, preferred_element_type=jnp.float32)
    hidden = (jax.nn.silu(gate) * upper).astype(jnp.bfloat16)
    full_hidden = lax.all_gather(hidden, "tensor", axis=1, tiled=True)
    summed = lax.psum_scatter(
        jnp.dot(full_hidden, down_rows, preferred_element_type=jnp.float32),
        "section",
        scatter_dimension=0,
        tiled=True,
    )
    returned = lax.all_to_all(
        summed.astype(jnp.bfloat16), "expert", split_axis=0, concat_axis=0, tiled=True
    )
    result = jnp.einsum("tc,cd->td", placing, returned, preferred_element_type=jnp.float32)
    return result.astype(jnp.bfloat16)


def solution(mesh):
    in_specs = (
        P(("section", "expert"), "tensor"),
        P("tensor"),
        P("tensor", None),
        P(("section", "expert"), None),
        P("expert", None, ("section", "tensor")),
        P("expert", None, ("section", "tensor")),
        P("expert", "section", "tensor"),
    )
    out_specs = P(("section", "expert"), "tensor")
    return jax.shard_map(
        on_device, mesh=mesh, in_specs=in_specs, out_specs=out_specs, check_vma=False
    )
```

profile of v0, /device:TPU:0, one launch (start us, length us, event | category | flops | bytes accessed | tf_op | source)
XLA Modules:
  0.0 360.6 jit_solution(11621119919947402343)
XLA Ops:
  6.5 0.0 copy-start
  6.5 0.0 copy-start.1
  6.5 0.0 copy-start.2
  6.5 0.0 copy-start.3
  6.5 0.0 all-gather.4.cloned.1.call-start
  6.6 1.4 fusion.8
  7.9 5.9 %psum.14 = f32[128,1]{0,1:T(1,128)S(1)} all-reduce(f32[128,1]{0,1:T(1,128)S(1)} %bitcast.37), channel_id=1, replica_groups=mesh['section'=4,'expert'=4,'tensor'=2] {'tensor'}, use_global_device_ids=true, to_apply=%region_3.0 | all-reduce | flops 128 | bytes 1024 | tf_op jit(solution)/shard_map/psum | solution.py:31
  13.8 0.0 copy-done
  13.9 1.5 fusion.12
  15.3 9.4 %psum.15 = f32[128,4]{1,0:T(8,128)S(1)} all-reduce(f32[128,4]{1,0:T(8,128)S(1)} %fusion.12), channel_id=1, replica_groups=mesh['section'=4,'expert'=4,'tensor'=2] {'tensor'}, use_global_device_ids=true, to_apply=%region_4.5 | all-reduce | flops 512 | bytes 4096 | tf_op jit(solution)/shard_map/psum | solution.py:33
  24.7 0.0 copy-done.3
  24.7 0.1 fusion.17
  24.8 0.2 select_reduce_fusion
  25.0 0.2 reduce_window_sum.11
  25.2 0.2 select_reduce_fusion.1
  25.4 0.0 copy-done.1
  25.4 0.0 copy-done.2
  25.4 0.6 convolution_convert_fusion
  26.0 33.1 %all_to_all.24 = bf16[4,64,2560]{2,1,0:T(8,128)(2,1)} all-to-all(bf16[4,64,2560]{2,1,0:T(8,128)(2,1)S(1)} %bitcast.31), channel_id=1, replica_groups=mesh['section'=4,'expert'=4,'tensor'=2] {'expert'}, dimensions={0} | all-to-all | bytes 2621440 | tf_op jit(solution)/shard_map/all_to_all | solution.py:41
  59.1 0.0 all-gather.4.cloned.1.call-update
  59.2 0.0 all-gather.6.cloned.1.call-start
  59.2 37.2 %all-gather.4.cloned.1.call-done = bf16[256,5120]{1,0:T(8,128)(2,1)} async-done(((bf16[256,2560]{1,0:T(8,128)(2,1)}), bf16[256,5120]{1,0:T(8,128)(2,1)}) %all-gather.4.cloned.1.call-update) | async-done | bytes 2621456 | tf_op jit(solution)/shard_map/all_gather | solution.py:45
  96.5 0.0 all-gather.6.cloned.1.call-update
  96.5 0.0 all-gather.8.cloned.1.call-start
  96.5 71.7 %all-gather.6.cloned.1.call-done = bf16[1024,5120]{1,0:T(8,128)(2,1)} async-done(((bf16[256,5120]{1,0:T(8,128)(2,1)}), bf16[1024,5120]{1,0:T(8,128)(2,1)}) %all-gather.6.cloned.1.call-update) | async-done | bytes 10485776 | tf_op jit(solution)/shard_map/all_gather | solution.py:46
  168.2 0.0 copy-start.4
  168.2 9.9 %fusion.2 = f32[1024,512]{1,0:T(8,128)S(1)} fusion(bf16[1024,5120]{1,0:T(8,128)(2,1)} %all-gather.6.cloned.1.call-done, bf16[1,5120,512]{2,1,0:T(8,128)(2,1)} %param.12), kind=kOutput, calls=%fused_computation.2 | convolution fusion | flops 5368709120 | bytes 17825792 | tf_op jit(solution)/shard_map/dot_general | solution.py:48
  178.2 0.0 copy-done.4
  178.2 8.4 %multiply_convert_fusion = bf16[1024,512]{1,0:T(8,128)(2,1)} fusion(f32[1024,512]{1,0:T(8,128)S(1)} %fusion.2, bf16[1024,5120]{1,0:T(8,128)(2,1)S(1)} %copy-done.4, bf16[1,5120,512]{2,1,0:T(8,128)(2,1)} %param.11), kind=kOutput, calls=%fused_computation.8 | convolution fusion | flops 5371854848 | bytes 18874368 | tf_op jit(solution)/shard_map/dot_general | solution.py:47
  186.6 0.0 all-gather.8.cloned.1.call-update
  186.6 0.0 reduce-scatter.2.cloned.1.call-start
  186.7 33.2 %all-gather.8.cloned.1.call-done = bf16[1024,1024]{1,0:T(8,128)(2,1)} async-done(((bf16[1024,512]{1,0:T(8,128)(2,1)}), bf16[1024,1024]{1,0:T(8,128)(2,1)}) %all-gather.8.cloned.1.call-update) | async-done | bytes 2097168 | tf_op jit(solution)/shard_map/all_gather | solution.py:50
  219.9 10.9 %fusion = f32[1024,2560]{1,0:T(8,128)} fusion(bf16[1024,1024]{1,0:T(8,128)(2,1)} %all-gather.8.cloned.1.call-done, bf16[1,1024,2560]{2,1,0:T(8,128)(2,1)} %param.13), kind=kOutput, calls=%fused_computation | convolution fusion | flops 5368709120 | bytes 17825792 | tf_op jit(solution)/shard_map/dot_general | solution.py:52
  230.8 0.0 reduce-scatter.2.cloned.1.call-update
  230.8 84.6 %reduce-scatter.2.cloned.1.call-done = f32[256,2560]{1,0:T(8,128)} async-done(((f32[1024,2560]{1,0:T(8,128)}), f32[256,2560]{1,0:T(8,128)}) %reduce-scatter.2.cloned.1.call-update) | async-done | bytes 2621456 | tf_op jit(solution)/shard_map/reduce_scatter | solution.py:51
  315.4 1.9 convert_element_type.36
  317.3 35.6 %all_to_all.25 = bf16[4,64,2560]{2,1,0:T(8,128)(2,1)S(1)} all-to-all(bf16[4,64,2560]{2,1,0:T(8,128)(2,1)S(1)} %bitcast.33), channel_id=1, replica_groups=mesh['section'=4,'expert'=4,'tensor'=2] {'expert'}, dimensions={0} | all-to-all | bytes 2621440 | tf_op jit(solution)/shard_map/all_to_all | solution.py:57
  352.9 1.2 convolution_convert_fusion.1
  (3 shorter events, 0.0 us)
Async XLA Ops:
  6.5 7.3 %copy-start = (bf16[2560,4]{0,1:T(4,128)(2,1)S(1)}, bf16[2560,4]{0,1:T(4,128)(2,1)}, u32[]{:S(2)}) copy-start(bf16[2560,4]{0,1:T(4,128)(2,1)} %param.9) | copy-start | bytes 61444
  6.5 18.8 %copy-start.1 = (bf16[128,2560]{1,0:T(8,128)(2,1)S(1)}, bf16[128,2560]{1,0:T(8,128)(2,1)}, u32[]{:S(2)}) copy-start(bf16[128,2560]{1,0:T(8,128)(2,1)} %param.7) | copy-start | bytes 1966084
  6.5 18.8 %copy-start.2 = (f32[2560]{0:T(1024)S(1)}, f32[2560]{0:T(1024)}, u32[]{:S(2)}) copy-start(f32[2560]{0:T(1024)} %param.8) | copy-start | bytes 30724
  6.5 18.2 %copy-start.3 = (s32[128,1]{0,1:T(1,128)S(1)}, s32[128,1]{0,1:T(1,128)}, u32[]{:S(2)}) copy-start(s32[128,1]{0,1:T(1,128)} %param.10) | copy-start | bytes 1540
  6.5 89.9 %all-gather.4.cloned.1.call-start = ((), (), s32[]{:S(2)}) async-start(), calls=%async_computation.3 | async-start | bytes 3932160 | tf_op jit(solution)/shard_map/all_gather | solution.py:45
  59.2 109.0 %all-gather.6.cloned.1.call-start = ((), (), s32[]{:S(2)}) async-start(), calls=%async_computation.4 | async-start | bytes 13107200 | tf_op jit(solution)/shard_map/all_gather | solution.py:46
  96.5 123.4 %all-gather.8.cloned.1.call-start = ((), (), s32[]{:S(2)}) async-start(), calls=%async_computation.5 | async-start | bytes 3145728 | tf_op jit(solution)/shard_map/all_gather | solution.py:50
  168.2 10.0 %copy-start.4 = (bf16[1024,5120]{1,0:T(8,128)(2,1)S(1)}, bf16[1024,5120]{1,0:T(8,128)(2,1)}, u32[]{:S(2)}) copy-start(bf16[1024,5120]{1,0:T(8,128)(2,1)} %all-gather.6.cloned.1.call-done) | copy-start | bytes 31457284
  186.6 128.8 %reduce-scatter.2.cloned.1.call-start = ((), (), s32[]{:S(2)}) async-start(), calls=%async_computation.6 | async-start | bytes 13107200 | tf_op jit(solution)/shard_map/reduce_scatter | solution.py:51
Sparse Core Ops, SparseCore 0:
  59.3 37.1 all-gather.3
  98.0 70.1 all-gather.5
  186.8 33.0 all-gather.7
  231.0 84.3 reduce-scatter.1
where the time goes:
time: 361 us
  waiting for transfers between devices  227 us (63%)
  blocking collectives  83.9 us (23%)
  matrix products  32.7 us (9%)
  between operations  13.2 us (4%)
  other arithmetic  3.86 us (1%)
    reduce_scatter x1, waiting for transfers between devices, on_device(): lax.psum_scatter(jnp.dot(full_hidden, down_rows, preferred_element_type=j...  84.6 us
    all_gather x1, waiting for transfers between devices, on_device(): piece = lax.all_gather(widened, 'section', axis=0, tiled=True)  71.7 us
    all_gather x1, waiting for transfers between devices, on_device(): widened = lax.all_gather(arrived, 'tensor', axis=1, tiled=True)  37.2 us
    all_to_all x1, blocking collectives, on_device(): lax.all_to_all(summed.astype(jnp.bfloat16), 'expert', split_axis=0, conca...  35.6 us
    all_gather x1, waiting for transfers between devices, on_device(): full_hidden = lax.all_gather(hidden, 'tensor', axis=1, tiled=True)  33.2 us
    all_to_all x1, blocking collectives, on_device(): lax.all_to_all(outgoing, 'expert', split_axis=0, concat_axis=0, tiled=True)  33.1 us
    dot_general x1, matrix products, on_device(): jnp.dot(full_hidden, down_rows, preferred_element_type=jnp.float32)  10.9 us
    dot_general x1, matrix products, on_device(): upper = jnp.dot(piece, up_cols, preferred_element_type=jnp.float32)  9.94 us
  transfers between devices with their start and end apart: 4, of which 4 were waited for; matrix products, arithmetic and copies ran while one was open for 0% of the time, Pallas kernels for 0%

commit v1 on v0

v1 whole, which is shorter than its diff:
```python
import functools

import jax
import jax.numpy as jnp
from jax import lax
from jax.experimental import pallas as pl
from jax.experimental.pallas import tpu as pltpu
from jax.sharding import PartitionSpec as P

EPSILON = 1e-05
CORES = 2
LANES = 128
MESH = pl.DeviceIdType.MESH


def tile_of(width):
    for tile in (512, 256, 128):
        if width % tile == 0:
            return tile
    return width


def sublayer(
    sections, experts, tensors, tokens_ref, gain_ref, router_ref, ids_ref, gate_hbm, up_hbm, down_hbm,
    out_ref, gate_w, up_w, down_w, stats, placing_ref, outgoing, piece, hidden, part, pair_in, cross_out,
    cross_in, back_out, back_in, weight_sem, stats_s, stats_r, out_s, piece_r, core_s, relay_s, px_s,
    pt_s, hid_s, hid_r, pair_s, pair_r, cross_s, cross_r, back_s, back_r,
):
    s, e, t = lax.axis_index("section"), lax.axis_index("expert"), lax.axis_index("tensor")
    x, c = lax.div(s, CORES), lax.rem(s, CORES)
    xs = sections // CORES
    rows, feats = tokens_ref.shape
    width = gate_hbm.shape[1]
    units = gate_hbm.shape[2]
    cap = outgoing.shape[0] // experts
    partner = s + 1 - 2 * c

    def other_x(k):
        return lax.rem(x + k, xs)

    def other_t(k):
        return lax.rem(t + k, tensors)

    def sec(xx, cc):
        return xx * CORES + cc

    def dev(ss, ee, tt):
        return {"section": ss, "expert": ee, "tensor": tt}

    barrier = pltpu.get_barrier_semaphore()
    peers = [dev(partner, e, t)]
    peers += [dev(sec(other_x(k), c), e, t) for k in range(1, xs)]
    peers += [dev(s, e, other_t(k)) for k in range(1, tensors)]
    peers += [dev(s, lax.rem(e + k, experts), t) for k in range(1, experts)]
    for peer in peers:
        pl.semaphore_signal(barrier, inc=1, device_id=peer, device_id_type=MESH)

    loads = [
        pltpu.make_async_copy(gate_hbm.at[0], gate_w, weight_sem.at[0]),
        pltpu.make_async_copy(up_hbm.at[0], up_w, weight_sem.at[1]),
        pltpu.make_async_copy(down_hbm.at[0], down_w, weight_sem.at[2]),
    ]
    for load in loads:
        load.start()

    ft = tile_of(feats)

    def span(n, tile):
        return pl.ds(pl.multiple_of(n * tile, LANES), tile)

    def gather_stats(n, carry):
        squares, logits = carry
        values = tokens_ref[:, span(n, ft)].astype(jnp.float32)
        scaled = (values * gain_ref[:, span(n, ft)]).astype(jnp.bfloat16)
        logits += jnp.dot(
            scaled, router_ref[pl.ds(pl.multiple_of(n * ft, LANES), ft), :],
            preferred_element_type=jnp.float32,
        )
        return squares + jnp.sum(values * values, axis=1, keepdims=True), logits

    squares, logits = lax.fori_loop(
        0, feats // ft, gather_stats,
        (jnp.zeros((rows, 1), jnp.float32), jnp.zeros((rows, LANES), jnp.float32)),
    )
    lane = lax.broadcasted_iota(jnp.int32, (rows, LANES), 1)
    stats[t] = jnp.where(lane == experts, squares, logits)
    pl.semaphore_wait(barrier, len(peers))

    def stats_copy(k):
        return pltpu.make_async_remote_copy(
            stats.at[t], stats.at[t], stats_s.at[k], stats_r.at[t],
            device_id=dev(s, e, other_t(k)), device_id_type=MESH,
        )

    for k in range(1, tensors):
        stats_copy(k).start()

    chosen = ids_ref[...]
    member = chosen == lane
    member_f = jnp.where(member, 1.0, 0.0).astype(jnp.float32)
    before = (
        lax.broadcasted_iota(jnp.int32, (rows, rows), 1) < lax.broadcasted_iota(jnp.int32, (rows, rows), 0)
    )
    earlier = jnp.dot(
        jnp.where(before, 1.0, 0.0).astype(jnp.bfloat16), member_f.astype(jnp.bfloat16),
        preferred_element_type=jnp.float32,
    )
    slot = jnp.sum(earlier * member_f, axis=1, keepdims=True)
    placed = chosen.astype(jnp.float32) * cap + slot
    places = lax.broadcasted_iota(jnp.int32, (rows, experts * cap), 1).astype(jnp.float32)
    placing_ref[...] = jnp.where(placed == places, 1.0, 0.0).astype(jnp.bfloat16)

    for k in range(1, tensors):
        pltpu.make_async_remote_copy(
            stats.at[t], stats.at[other_t(k)], stats_s.at[k], stats_r.at[other_t(k)],
            device_id=dev(s, e, other_t(k)), device_id_type=MESH,
        ).wait_recv()
    total = stats[0]
    for k in range(1, tensors):
        total += stats[k]
    squares = jnp.sum(jnp.where(lane == experts, total, 0.0), axis=1, keepdims=True)
    inverse = lax.rsqrt(squares / width + EPSILON)
    score = jax.nn.sigmoid(jnp.sum(total * member_f, axis=1, keepdims=True) * inverse)

    @pl.loop(0, feats // ft)
    def _(n):
        values = tokens_ref[:, span(n, ft)].astype(jnp.float32)
        normed = (values * inverse * gain_ref[:, span(n, ft)]).astype(jnp.bfloat16)
        routed = (normed.astype(jnp.float32) * score).astype(jnp.bfloat16)
        outgoing[:, span(n, ft)] = lax.dot_general(
            placing_ref[...], routed, (((0,), (0,)), ((), ())), preferred_element_type=jnp.float32
        ).astype(jnp.bfloat16)

    def group_rows(index):
        return pl.ds(pl.multiple_of(index * cap, cap), cap)

    def block(z, ss, tt):
        return piece.at[z, group_rows(ss), pl.ds(pl.multiple_of(tt * feats, LANES), feats)]

    def chunk_copy(z, ss, tt, send_sem, to):
        return pltpu.make_async_remote_copy(
            block(z, ss, tt), block(z, ss, tt), send_sem, piece_r.at[z, ss, tt],
            device_id=to, device_id_type=MESH,
        )

    def out_copy(k):
        target = lax.rem(e + k, experts)
        return pltpu.make_async_remote_copy(
            outgoing.at[group_rows(target)], block(e, s, t), out_s.at[k], piece_r.at[e, s, t],
            device_id=dev(s, target, t), device_id_type=MESH,
        )

    own = pltpu.make_async_copy(outgoing.at[group_rows(e)], block(e, s, t), piece_r.at[e, s, t])
    own.start()
    for k in range(1, experts):
        out_copy(k).start()

    def source(i):
        return lax.rem(e + experts - i, experts)

    to_partner = dev(partner, e, t)

    def arrived(z, ss, tt):
        chunk_copy(z, ss, tt, core_s.at[0, 0, 0], to_partner).wait_recv()

    def core_copy(i, xx, tt):
        return chunk_copy(source(i), sec(xx, c), tt, core_s.at[i, xx, tt], to_partner)

    def px_copy(i, k):
        return chunk_copy(source(i), s, t, px_s.at[i, k], dev(sec(other_x(k), c), e, t))

    def pt_copy(i, k):
        return chunk_copy(source(i), s, t, pt_s.at[i, k], dev(s, e, other_t(k)))

    def relay_t_copy(i, kx, kt):
        return chunk_copy(
            source(i), sec(other_x(kx), c), t, relay_s.at[i, kx, kt], dev(s, e, other_t(kt))
        )

    def relay_x_copy(i, kx, kt):
        return chunk_copy(
            source(i), s, other_t(kt), relay_s.at[i, kx, kt], dev(sec(other_x(kx), c), e, t)
        )

    def push(i):
        arrived(source(i), s, t)
        for k in range(1, xs):
            px_copy(i, k).start()
        for k in range(1, tensors):
            pt_copy(i, k).start()
        core_copy(i, x, t).start()

    def relay(i):
        even = lax.rem(i, 2) == 0
        for kx in range(1, xs):
            arrived(source(i), sec(other_x(kx), c), t)

            @pl.when(even)
            def _():
                for kt in range(1, tensors):
                    relay_t_copy(i, kx, kt).start()

            core_copy(i, other_x(kx), t).start()
        for kt in range(1, tensors):
            arrived(source(i), s, other_t(kt))

            @pl.when(jnp.logical_not(even))
            def _():
                for kx in range(1, xs):
                    relay_x_copy(i, kx, kt).start()

            core_copy(i, x, other_t(kt)).start()

    def hid_block(i, tt):
        return hidden.at[i, :, pl.ds(pl.multiple_of(tt * units, LANES), units)]

    def hid_copy(i, k):
        return pltpu.make_async_remote_copy(
            hid_block(i, t), hid_block(i, t), hid_s.at[i, k], hid_r.at[i, t],
            device_id=dev(s, e, other_t(k)), device_id_type=MESH,
        )

    ut = min(256, units)

    def expand(i):
        z = source(i)
        for kx in range(1, xs):
            for kt in range(1, tensors):
                arrived(z, sec(other_x(kx), c), other_t(kt))
                core_copy(i, other_x(kx), other_t(kt)).start()
        for xx in range(xs):
            for tt in range(tensors):
                arrived(z, sec(xx, 1 - c), tt)

        @pl.when(i == 0)
        def _():
            loads[0].wait()
            loads[1].wait()
            loads[2].wait()

        @pl.loop(0, units // ut)
        def _(n):
            gate = jnp.dot(piece[z], gate_w[:, span(n, ut)], preferred_element_type=jnp.float32)
            upper = jnp.dot(piece[z], up_w[:, span(n, ut)], preferred_element_type=jnp.float32)
            hidden[i, :, pl.ds(pl.multiple_of(t * units + n * ut, LANES), ut)] = (
                jax.nn.silu(gate) * upper
            ).astype(jnp.bfloat16)

        for k in range(1, tensors):
            hid_copy(i, k).start()

    def pair_copy(i, xx):
        return pltpu.make_async_remote_copy(
            part.at[i, group_rows(sec(xx, 1 - c))], pair_in.at[i, xx], pair_s.at[i, xx], pair_r.at[i, xx],
            device_id=to_partner, device_id_type=MESH,
        )

    def contract(i):
        for k in range(1, tensors):
            pltpu.make_async_remote_copy(
                hid_block(i, t), hid_block(i, other_t(k)), hid_s.at[i, k], hid_r.at[i, other_t(k)],
                device_id=dev(s, e, other_t(k)), device_id_type=MESH,
            ).wait_recv()

        @pl.loop(0, feats // ft)
        def _(n):
            part[i, :, span(n, ft)] = jnp.dot(
                hidden[i], down_w[:, span(n, ft)], preferred_element_type=jnp.float32
            ).astype(jnp.bfloat16)

        for xx in range(xs):
            pair_copy(i, xx).start()

    def cross_copy(i, k):
        return pltpu.make_async_remote_copy(
            cross_out.at[i, k - 1], cross_in.at[i, k - 1], cross_s.at[i, k], cross_r.at[i, k],
            device_id=dev(sec(other_x(k), c), e, t), device_id_type=MESH,
        )

    def pair_sum(i, xx, n):
        mine = part[i, group_rows(sec(xx, c)), span(n, ft)].astype(jnp.float32)
        return mine + pair_in[i, xx, :, span(n, ft)].astype(jnp.float32)

    def cross(i):
        for xx in range(xs):
            pair_copy(i, xx).wait_recv()
        for k in range(1, xs):

            @pl.loop(0, feats // ft)
            def _(n):
                cross_out[i, k - 1, :, span(n, ft)] = pair_sum(i, other_x(k), n).astype(jnp.bfloat16)

            cross_copy(i, k).start()

    def back_copy(i):
        return pltpu.make_async_remote_copy(
            back_out.at[i], back_in.at[group_rows(e)], back_s.at[i], back_r.at[e],
            device_id=dev(s, source(i), t), device_id_type=MESH,
        )

    own_back = pltpu.make_async_copy(back_out.at[0], back_in.at[group_rows(e)], back_r.at[e])

    def finish(i):
        for k in range(1, xs):
            cross_copy(i, k).wait_recv()

        @pl.loop(0, feats // ft)
        def _(n):
            total = pair_sum(i, x, n)
            for k in range(1, xs):
                total += cross_in[i, k - 1, :, span(n, ft)].astype(jnp.float32)
            back_out[i, :, span(n, ft)] = total.astype(jnp.bfloat16)

        @pl.when(i == 0)
        def _():
            own_back.start()

        @pl.when(i > 0)
        def _():
            back_copy(i).start()

        for xx in range(xs):
            for tt in range(tensors):
                core_copy(i, xx, tt).wait_send()
            pair_copy(i, xx).wait_send()
        for k in range(1, xs):
            px_copy(i, k).wait_send()
            cross_copy(i, k).wait_send()
        for k in range(1, tensors):
            pt_copy(i, k).wait_send()
            hid_copy(i, k).wait_send()
        for kx in range(1, xs):
            for kt in range(1, tensors):
                relay_t_copy(i, kx, kt).wait_send()

    stages = (push, relay, expand, contract, cross, finish)

    @pl.loop(0, experts + len(stages) - 1)
    def _(step):
        for lag, stage in enumerate(stages):

            @pl.when(jnp.logical_and(step >= lag, step < experts + lag))
            def _():
                stage(step - lag)

    own_back.wait()
    for k in range(1, tensors):
        stats_copy(k).wait_send()
    for k in range(1, experts):
        out_copy(k).wait_send()
        back_copy(k).wait_send()
        pltpu.make_async_remote_copy(
            back_out.at[k], back_in.at[group_rows(source(k))], back_s.at[k], back_r.at[source(k)],
            device_id=dev(s, source(k), t), device_id_type=MESH,
        ).wait_recv()

    @pl.loop(0, feats // ft)
    def _(n):
        out_ref[:, span(n, ft)] = jnp.dot(
            placing_ref[...], back_in[:, span(n, ft)], preferred_element_type=jnp.float32
        ).astype(jnp.bfloat16)


def on_device(sections, experts, tensors, tokens, norm_gain, router, expert_ids, gate_proj, up_proj, down_proj):
    rows, feats = tokens.shape
    cap = 2 * rows // experts
    width, units = gate_proj.shape[1:]
    depth = down_proj.shape[1]
    group = sections * cap
    xs = sections // CORES
    bf16 = jnp.bfloat16
    dma = pltpu.SemaphoreType.DMA
    vmem = pl.BlockSpec(memory_space=pltpu.VMEM)
    anywhere = pl.BlockSpec(memory_space=pl.ANY)
    router = jnp.pad(router, ((0, 0), (0, LANES - router.shape[1])))
    return pl.pallas_call(
        functools.partial(sublayer, sections, experts, tensors),
        out_shape=jax.ShapeDtypeStruct((rows, feats), bf16),
        in_specs=[vmem] * 4 + [anywhere] * 3,
        out_specs=vmem,
        scratch_shapes=[
            pltpu.VMEM((width, units), bf16),
            pltpu.VMEM((width, units), bf16),
            pltpu.VMEM((depth, feats), bf16),
            pltpu.VMEM((tensors, rows, LANES), jnp.float32),
            pltpu.VMEM((rows, experts * cap), bf16),
            pltpu.VMEM((experts * cap, feats), bf16),
            pltpu.VMEM((experts, group, width), bf16),
            pltpu.VMEM((experts, group, depth), bf16),
            pltpu.VMEM((experts, group, feats), bf16),
            pltpu.VMEM((experts, xs, cap, feats), bf16),
            pltpu.VMEM((experts, max(1, xs - 1), cap, feats), bf16),
            pltpu.VMEM((experts, max(1, xs - 1), cap, feats), bf16),
            pltpu.VMEM((experts, cap, feats), bf16),
            pltpu.VMEM((experts * cap, feats), bf16),
            dma((3,)),
            dma((tensors,)),
            dma((tensors,)),
            dma((experts,)),
            dma((experts, sections, tensors)),
            dma((experts, xs, tensors)),
            dma((experts, xs, tensors)),
            dma((experts, xs)),
            dma((experts, tensors)),
            dma((experts, tensors)),
            dma((experts, tensors)),
            dma((experts, xs)),
            dma((experts, xs)),
            dma((experts, xs)),
            dma((experts, xs)),
            dma((experts,)),
            dma((experts,)),
        ],
        compiler_params=pltpu.CompilerParams(
            collective_id=0, has_side_effects=True, vmem_limit_bytes=62 * 1024 * 1024
        ),
    )(tokens, norm_gain.reshape(1, feats), router, expert_ids, gate_proj, up_proj, down_proj)


def solution(mesh):
    in_specs = (
        P(("section", "expert"), "tensor"),
        P("tensor"),
        P("tensor", None),
        P(("section", "expert"), None),
        P("expert", None, ("section", "tensor")),
        P("expert", None, ("section", "tensor")),
        P("expert", "section", "tensor"),
    )
    body = functools.partial(on_device, *[mesh.shape[axis] for axis in ("section", "expert", "tensor")])
    return jax.shard_map(
        body, mesh=mesh, in_specs=in_specs, out_specs=P(("section", "expert"), "tensor"), check_vma=False
    )
```

time: 361 us -> 135 us (0.37)
  waiting for transfers between devices: 227 us -> 0 us
  Pallas kernels: 0 us -> 128 us
  blocking collectives: 83.9 us -> 0 us
  matrix products: 32.7 us -> 0 us
  between operations: 13.2 us -> 0.01 us
  local copies, waits for them, and re-layouts: 0.02 us -> 6.72 us
  other arithmetic: 3.86 us -> 0 us
    all_gather x3 -> x0, waiting for transfers between devices: 142 us -> none  [the longest x1 71.7 us: on_device(): piece = lax.all_gather(widened, 'section', axis=0, tiled=True)]
    pallas_call x0 -> x1, Pallas kernels: none -> 128 us  [on_device(): pl.pallas_call(functools.partial(sublayer, sections, experts, tensors), o...]
    reduce_scatter x1 -> x0, waiting for transfers between devices: 84.6 us -> none  [on_device(): lax.psum_scatter(jnp.dot(full_hidden, down_rows, preferred_element_type=j...]
    all_to_all x2 -> x0, blocking collectives: 68.7 us -> none  [the longest x1 35.6 us: on_device(): lax.all_to_all(summed.astype(jnp.bfloat16), 'expert', split_axis=0, conca...]
    dot_general x6 -> x0, matrix products: 32.7 us -> none  [the longest x1 10.9 us: on_device(): jnp.dot(full_hidden, down_rows, preferred_element_type=jnp.float32)]
    psum x2 -> x0, blocking collectives: 15.3 us -> none  [the longest x1 9.36 us: on_device(): lax.psum(jnp.dot(normed, router, preferred_element_type=jnp.float32), 'te...]
    unnamed x10 -> x3, local copies, waits for them, and re-layouts: 0.02 us -> 4.45 us
  transfers between devices with their start and end apart: 4 -> 0, of which waited for: 4 -> 0; matrix products, arithmetic and copies ran while one was open for 0% -> 0% of each run, Pallas kernels for 0% -> 0%
where the time goes in v1:
time: 135 us
  Pallas kernels  128 us (95%)
  local copies, waits for them, and re-layouts  6.72 us (5%)
    pallas_call x1, Pallas kernels, on_device(): pl.pallas_call(functools.partial(sublayer, sections, experts, tensors), o...  128 us
    unnamed x3, local copies, waits for them, and re-layouts  4.45 us

profile of v1, /device:TPU:0, one launch (start us, length us, event | category | flops | bytes accessed | tf_op | source)
XLA Modules:
  0.0 134.7 jit_solution(2295480194954569744)
XLA Ops:
  0.0 1.3 reshape.3.gain_ref
  1.3 1.4 %copy.9.ids_ref = s32[128,1]{1,0:T(8,128)} copy(s32[128,1]{0,1:T(1,128)} %param.10) | data formatting | bytes 1024 | tf_op args[3]
  2.7 1.1 copy.8
  3.8 1.0 pad.4.router_ref
  4.8 128.0 %shard_map.73 = bf16[128,2560]{1,0:T(8,128)(2,1)} custom-call(bf16[128,2560]{1,0:T(8,128)(2,1)} %tokens_ref.1, f32[1,2560]{1,0:T(1,128)} %reshape.3.gain_ref, bf16[2560,128]{1,0:T(8,128)(2,1)} %pad.4.router_ref, s32[128,1]{1,0:T(8,128)} %copy.9.ids_ref, bf16[1,5120,512]{2,1,0:T(8,128)(2,1)} %gate_hbm.1, bf16[1,5120,512]{2,1,0:T(8,128)(2,1)} %up_hbm.1, ...), custom_call_target="tpu_custom_call" | custom-call | tf_op jit(solution)/shard_map/pallas_call | solution.py:376
  132.8 2.0 %copy.11 = bf16[128,2560]{1,0:T(8,128)(2,1)} copy(bf16[128,2560]{1,0:T(8,128)(2,1)} %shard_map.73) | data formatting | bytes 1310720

commit v2 on v1

--- a/solution.py
+++ b/solution.py
@@ -10,6 +10,7 @@
 EPSILON = 1e-05
 CORES = 2
 LANES = 128
+HALVES = 2
 MESH = pl.DeviceIdType.MESH
 
 
@@ -32,7 +33,10 @@
     rows, feats = tokens_ref.shape
     width = gate_hbm.shape[1]
     units = gate_hbm.shape[2]
-    cap = outgoing.shape[0] // experts
+    groups = piece.shape[0]
+    halves = groups // experts
+    cap = outgoing.shape[0] // groups
+    slots = cap * halves
     partner = s + 1 - 2 * c
 
     def other_x(k):
@@ -71,19 +75,20 @@
     def gather_stats(n, carry):
         squares, logits = carry
         values = tokens_ref[:, span(n, ft)].astype(jnp.float32)
-        scaled = (values * gain_ref[:, span(n, ft)]).astype(jnp.bfloat16)
-        logits += jnp.dot(
-            scaled, router_ref[pl.ds(pl.multiple_of(n * ft, LANES), ft), :],
+        scaled = (values * gain_ref[span(n, ft)][None, :]).astype(jnp.bfloat16)
+        logits += lax.dot_general(
+            scaled, router_ref[:, span(n, ft)], (((1,), (1,)), ((), ())),
             preferred_element_type=jnp.float32,
         )
         return squares + jnp.sum(values * values, axis=1, keepdims=True), logits
 
     squares, logits = lax.fori_loop(
         0, feats // ft, gather_stats,
-        (jnp.zeros((rows, 1), jnp.float32), jnp.zeros((rows, LANES), jnp.float32)),
+        (jnp.zeros((rows, 1), jnp.float32), jnp.zeros((rows, experts), jnp.float32)),
     )
     lane = lax.broadcasted_iota(jnp.int32, (rows, LANES), 1)
-    stats[t] = jnp.where(lane == experts, squares, logits)
+    stats[t] = jnp.where(lane == experts, squares, 0.0)
+    stats[t, :, 0:experts] = logits
     pl.semaphore_wait(barrier, len(peers))
 
     def stats_copy(k):
@@ -95,19 +100,20 @@
     for k in range(1, tensors):
         stats_copy(k).start()
 
-    chosen = ids_ref[...]
+    across = lax.broadcasted_iota(jnp.int32, (rows, rows), 1)
+    down = lax.broadcasted_iota(jnp.int32, (rows, rows), 0)
+    chosen = jnp.sum(jnp.where(across == down, ids_ref[...].astype(jnp.float32), 0.0), axis=1, keepdims=True)
+    chosen = chosen.astype(jnp.int32)
     member = chosen == lane
     member_f = jnp.where(member, 1.0, 0.0).astype(jnp.float32)
-    before = (
-        lax.broadcasted_iota(jnp.int32, (rows, rows), 1) < lax.broadcasted_iota(jnp.int32, (rows, rows), 0)
-    )
+    before = across < down
     earlier = jnp.dot(
         jnp.where(before, 1.0, 0.0).astype(jnp.bfloat16), member_f.astype(jnp.bfloat16),
         preferred_element_type=jnp.float32,
     )
     slot = jnp.sum(earlier * member_f, axis=1, keepdims=True)
-    placed = chosen.astype(jnp.float32) * cap + slot
-    places = lax.broadcasted_iota(jnp.int32, (rows, experts * cap), 1).astype(jnp.float32)
+    placed = chosen.astype(jnp.float32) * slots + slot
+    places = lax.broadcasted_iota(jnp.int32, (rows, experts * slots), 1).astype(jnp.float32)
     placing_ref[...] = jnp.where(placed == places, 1.0, 0.0).astype(jnp.bfloat16)
 
     for k in range(1, tensors):
@@ -125,7 +131,7 @@
     @pl.loop(0, feats // ft)
     def _(n):
         values = tokens_ref[:, span(n, ft)].astype(jnp.float32)
-        normed = (values * inverse * gain_ref[:, span(n, ft)]).astype(jnp.bfloat16)
+        normed = (values * inverse * gain_ref[span(n, ft)][None, :]).astype(jnp.bfloat16)
         routed = (normed.astype(jnp.float32) * score).astype(jnp.bfloat16)
         outgoing[:, span(n, ft)] = lax.dot_general(
             placing_ref[...], routed, (((0,), (0,)), ((), ())), preferred_element_type=jnp.float32
@@ -143,20 +149,28 @@
             device_id=to, device_id_type=MESH,
         )
 
-    def out_copy(k):
-        target = lax.rem(e + k, experts)
-        return pltpu.make_async_remote_copy(
-            outgoing.at[group_rows(target)], block(e, s, t), out_s.at[k], piece_r.at[e, s, t],
+    def out_copy(i):
+        target = lax.rem(e + lax.div(i, halves), experts)
+        h = lax.rem(i, halves)
+        return pltpu.make_async_remote_copy(
+            outgoing.at[group_rows(target * halves + h)], block(e * halves + h, s, t), out_s.at[i],
+            piece_r.at[e * halves + h, s, t],
             device_id=dev(s, target, t), device_id_type=MESH,
         )
 
-    own = pltpu.make_async_copy(outgoing.at[group_rows(e)], block(e, s, t), piece_r.at[e, s, t])
-    own.start()
-    for k in range(1, experts):
-        out_copy(k).start()
+    for h in range(halves):
+        z = e * halves + h
+        pltpu.make_async_copy(outgoing.at[group_rows(z)], block(z, s, t), piece_r.at[z, s, t]).start()
+
+    @pl.loop(halves, groups)
+    def _(i):
+        out_copy(i).start()
+
+    def owner(i):
+        return lax.rem(e + experts - lax.div(i, halves), experts)
 
     def source(i):
-        return lax.rem(e + experts - i, experts)
+        return owner(i) * halves + lax.rem(i, halves)
 
     to_partner = dev(partner, e, t)
 
@@ -211,16 +225,17 @@
 
             core_copy(i, x, other_t(kt)).start()
 
-    def hid_block(i, tt):
-        return hidden.at[i, :, pl.ds(pl.multiple_of(tt * units, LANES), units)]
-
-    def hid_copy(i, k):
-        return pltpu.make_async_remote_copy(
-            hid_block(i, t), hid_block(i, t), hid_s.at[i, k], hid_r.at[i, t],
+    ut = min(256, units)
+
+    def hid_block(i, tt, n):
+        return hidden.at[i, :, pl.ds(pl.multiple_of(tt * units + n * ut, LANES), ut)]
+
+    def hid_copy(i, k, n):
+        return pltpu.make_async_remote_copy(
+            hid_block(i, t, n), hid_block(i, t, n), hid_s.at[i, k, n], hid_r.at[i, t, n],
             device_id=dev(s, e, other_t(k)), device_id_type=MESH,
         )
 
-    ut = min(256, units)
 
     def expand(i):
         z = source(i)
@@ -245,35 +260,36 @@
             hidden[i, :, pl.ds(pl.multiple_of(t * units + n * ut, LANES), ut)] = (
                 jax.nn.silu(gate) * upper
             ).astype(jnp.bfloat16)
-
-        for k in range(1, tensors):
-            hid_copy(i, k).start()
-
-    def pair_copy(i, xx):
-        return pltpu.make_async_remote_copy(
-            part.at[i, group_rows(sec(xx, 1 - c))], pair_in.at[i, xx], pair_s.at[i, xx], pair_r.at[i, xx],
+            for k in range(1, tensors):
+                hid_copy(i, k, n).start()
+
+    def pair_copy(i, xx, n):
+        return pltpu.make_async_remote_copy(
+            part.at[i, group_rows(sec(xx, 1 - c)), span(n, ft)], pair_in.at[i, xx, :, span(n, ft)],
+            pair_s.at[i, xx, n], pair_r.at[i, xx, n],
             device_id=to_partner, device_id_type=MESH,
         )
 
     def contract(i):
         for k in range(1, tensors):
-            pltpu.make_async_remote_copy(
-                hid_block(i, t), hid_block(i, other_t(k)), hid_s.at[i, k], hid_r.at[i, other_t(k)],
-                device_id=dev(s, e, other_t(k)), device_id_type=MESH,
-            ).wait_recv()
+            for n in range(units // ut):
+                pltpu.make_async_remote_copy(
+                    hid_block(i, t, n), hid_block(i, other_t(k), n), hid_s.at[i, k, n],
+                    hid_r.at[i, other_t(k), n], device_id=dev(s, e, other_t(k)), device_id_type=MESH,
+                ).wait_recv()
 
         @pl.loop(0, feats // ft)
         def _(n):
             part[i, :, span(n, ft)] = jnp.dot(
                 hidden[i], down_w[:, span(n, ft)], preferred_element_type=jnp.float32
             ).astype(jnp.bfloat16)
-
-        for xx in range(xs):
-            pair_copy(i, xx).start()
-
-    def cross_copy(i, k):
-        return pltpu.make_async_remote_copy(
-            cross_out.at[i, k - 1], cross_in.at[i, k - 1], cross_s.at[i, k], cross_r.at[i, k],
+            for xx in range(xs):
+                pair_copy(i, xx, n).start()
+
+    def cross_copy(i, k, n):
+        return pltpu.make_async_remote_copy(
+            cross_out.at[i, k - 1, :, span(n, ft)], cross_in.at[i, k - 1, :, span(n, ft)],
+            cross_s.at[i, k, n], cross_r.at[i, k, n],
             device_id=dev(sec(other_x(k), c), e, t), device_id_type=MESH,
         )
 
@@ -282,77 +298,95 @@
         return mine + pair_in[i, xx, :, span(n, ft)].astype(jnp.float32)
 
     def cross(i):
-        for xx in range(xs):
-            pair_copy(i, xx).wait_recv()
-        for k in range(1, xs):
-
-            @pl.loop(0, feats // ft)
-            def _(n):
-                cross_out[i, k - 1, :, span(n, ft)] = pair_sum(i, other_x(k), n).astype(jnp.bfloat16)
-
-            cross_copy(i, k).start()
-
-    def back_copy(i):
-        return pltpu.make_async_remote_copy(
-            back_out.at[i], back_in.at[group_rows(e)], back_s.at[i], back_r.at[e],
-            device_id=dev(s, source(i), t), device_id_type=MESH,
-        )
-
-    own_back = pltpu.make_async_copy(back_out.at[0], back_in.at[group_rows(e)], back_r.at[e])
-
-    def finish(i):
-        for k in range(1, xs):
-            cross_copy(i, k).wait_recv()
-
         @pl.loop(0, feats // ft)
         def _(n):
+            for xx in range(xs):
+                pair_copy(i, xx, n).wait_recv()
+            for k in range(1, xs):
+                cross_out[i, k - 1, :, span(n, ft)] = pair_sum(i, other_x(k), n).astype(jnp.bfloat16)
+                cross_copy(i, k, n).start()
+
+    def back_copy(i, n):
+        return pltpu.make_async_remote_copy(
+            back_out.at[i, :, span(n, ft)], back_in.at[group_rows(e * halves + lax.rem(i, halves)), span(n, ft)],
+            back_s.at[i, n], back_r.at[e * halves + lax.rem(i, halves), n],
+            device_id=dev(s, owner(i), t), device_id_type=MESH,
+        )
+
+    def own_back(i, n):
+        return pltpu.make_async_copy(
+            back_out.at[i, :, span(n, ft)], back_in.at[group_rows(e * halves + i), span(n, ft)],
+            back_r.at[e * halves + i, n],
+        )
+
+    def finish(i):
+        @pl.loop(0, feats // ft)
+        def _(n):
+            for k in range(1, xs):
+                cross_copy(i, k, n).wait_recv()
             total = pair_sum(i, x, n)
             for k in range(1, xs):
                 total += cross_in[i, k - 1, :, span(n, ft)].astype(jnp.float32)
             back_out[i, :, span(n, ft)] = total.astype(jnp.bfloat16)
 
-        @pl.when(i == 0)
-        def _():
-            own_back.start()
-
-        @pl.when(i > 0)
-        def _():
-            back_copy(i).start()
-
+            @pl.when(i < halves)
+            def _():
+                own_back(i, n).start()
+
+            @pl.when(i >= halves)
+            def _():
+                back_copy(i, n).start()
+
+    def settle(i):
         for xx in range(xs):
             for tt in range(tensors):
                 core_copy(i, xx, tt).wait_send()
-            pair_copy(i, xx).wait_send()
         for k in range(1, xs):
             px_copy(i, k).wait_send()
-            cross_copy(i, k).wait_send()
         for k in range(1, tensors):
             pt_copy(i, k).wait_send()
-            hid_copy(i, k).wait_send()
+            for n in range(units // ut):
+                hid_copy(i, k, n).wait_send()
         for kx in range(1, xs):
             for kt in range(1, tensors):
                 relay_t_copy(i, kx, kt).wait_send()
-
-    stages = (push, relay, expand, contract, cross, finish)
-
-    @pl.loop(0, experts + len(stages) - 1)
+        for n in range(feats // ft):
+            for xx in range(xs):
+                pair_copy(i, xx, n).wait_send()
+            for k in range(1, xs):
+                cross_copy(i, k, n).wait_send()
+
+    stages = ((1, relay), (0, push), (2, expand), (3, contract), (4, cross), (5, finish))
+
+    @pl.loop(0, groups + len(stages) - 1)
     def _(step):
-        for lag, stage in enumerate(stages):
-
-            @pl.when(jnp.logical_and(step >= lag, step < experts + lag))
+        for lag, stage in stages:
+
+            @pl.when(jnp.logical_and(step >= lag, step < groups + lag))
             def _():
                 stage(step - lag)
 
-    own_back.wait()
+    @pl.loop(0, groups)
+    def _(i):
+        settle(i)
+
+    @pl.loop(0, halves)
+    def _(i):
+        for n in range(feats // ft):
+            own_back(i, n).wait()
+
     for k in range(1, tensors):
         stats_copy(k).wait_send()
-    for k in range(1, experts):
-        out_copy(k).wait_send()
-        back_copy(k).wait_send()
-        pltpu.make_async_remote_copy(
-            back_out.at[k], back_in.at[group_rows(source(k))], back_s.at[k], back_r.at[source(k)],
-            device_id=dev(s, source(k), t), device_id_type=MESH,
-        ).wait_recv()
+
+    @pl.loop(halves, groups)
+    def _(i):
+        out_copy(i).wait_send()
+        for n in range(feats // ft):
+            back_copy(i, n).wait_send()
+            pltpu.make_async_remote_copy(
+                back_out.at[i, :, span(n, ft)], back_in.at[group_rows(source(i)), span(n, ft)],
+                back_s.at[i, n], back_r.at[source(i), n], device_id=dev(s, owner(i), t), device_id_type=MESH,
+            ).wait_recv()
 
     @pl.loop(0, feats // ft)
     def _(n):
@@ -363,7 +397,10 @@
 
 def on_device(sections, experts, tensors, tokens, norm_gain, router, expert_ids, gate_proj, up_proj, down_proj):
     rows, feats = tokens.shape
-    cap = 2 * rows // experts
+    slots = 2 * rows // experts
+    halves = HALVES if slots % (16 * HALVES) == 0 else 1
+    cap = slots // halves
+    groups = experts * halves
     width, units = gate_proj.shape[1:]
     depth = down_proj.shape[1]
     group = sections * cap
@@ -372,7 +409,8 @@
     dma = pltpu.SemaphoreType.DMA
     vmem = pl.BlockSpec(memory_space=pltpu.VMEM)
     anywhere = pl.BlockSpec(memory_space=pl.ANY)
-    router = jnp.pad(router, ((0, 0), (0, LANES - router.shape[1])))
+    pieces = feats // tile_of(feats)
+    tiles = units // min(256, units)
     return pl.pallas_call(
         functools.partial(sublayer, sections, experts, tensors),
         out_shape=jax.ShapeDtypeStruct((rows, feats), bf16),
@@ -383,38 +421,38 @@
             pltpu.VMEM((width, units), bf16),
             pltpu.VMEM((depth, feats), bf16),
             pltpu.VMEM((tensors, rows, LANES), jnp.float32),
-            pltpu.VMEM((rows, experts * cap), bf16),
-            pltpu.VMEM((experts * cap, feats), bf16),
-            pltpu.VMEM((experts, group, width), bf16),
-            pltpu.VMEM((experts, group, depth), bf16),
-            pltpu.VMEM((experts, group, feats), bf16),
-            pltpu.VMEM((experts, xs, cap, feats), bf16),
-            pltpu.VMEM((experts, max(1, xs - 1), cap, feats), bf16),
-            pltpu.VMEM((experts, max(1, xs - 1), cap, feats), bf16),
-            pltpu.VMEM((experts, cap, feats), bf16),
-            pltpu.VMEM((experts * cap, feats), bf16),
+            pltpu.VMEM((rows, groups * cap), bf16),
+            pltpu.VMEM((groups * cap, feats), bf16),
+            pltpu.VMEM((groups, group, width), bf16),
+            pltpu.VMEM((groups, group, depth), bf16),
+            pltpu.VMEM((groups, group, feats), bf16),
+            pltpu.VMEM((groups, xs, cap, feats), bf16),
+            pltpu.VMEM((groups, max(1, xs - 1), cap, feats), bf16),
+            pltpu.VMEM((groups, max(1, xs - 1), cap, feats), bf16),
+            pltpu.VMEM((groups, cap, feats), bf16),
+            pltpu.VMEM((groups * cap, feats), bf16),
             dma((3,)),
             dma((tensors,)),
             dma((tensors,)),
-            dma((experts,)),
-            dma((experts, sections, tensors)),
-            dma((experts, xs, tensors)),
-            dma((experts, xs, tensors)),
-            dma((experts, xs)),
-            dma((experts, tensors)),
-            dma((experts, tensors)),
-            dma((experts, tensors)),
-            dma((experts, xs)),
-            dma((experts, xs)),
-            dma((experts, xs)),
-            dma((experts, xs)),
-            dma((experts,)),
-            dma((experts,)),
+            dma((groups,)),
+            dma((groups, sections, tensors)),
+            dma((groups, xs, tensors)),
+            dma((groups, xs, tensors)),
+            dma((groups, xs)),
+            dma((groups, tensors)),
+            dma((groups, tensors, tiles)),
+            dma((groups, tensors, tiles)),
+            dma((groups, xs, pieces)),
+            dma((groups, xs, pieces)),
+            dma((groups, xs, pieces)),
+            dma((groups, xs, pieces)),
+            dma((groups, pieces)),
+            dma((groups, pieces)),
         ],
         compiler_params=pltpu.CompilerParams(
             collective_id=0, has_side_effects=True, vmem_limit_bytes=62 * 1024 * 1024
         ),
-    )(tokens, norm_gain.reshape(1, feats), router, expert_ids, gate_proj, up_proj, down_proj)
+    )(tokens, norm_gain, router.T, expert_ids.reshape(1, rows), gate_proj, up_proj, down_proj)
 
 
 def solution(mesh):

time: 135 us -> 116 us (0.86)
  Pallas kernels: 128 us -> 114 us
  local copies, waits for them, and re-layouts: 6.72 us -> 1.97 us
    pallas_call x1, Pallas kernels: 128 us -> 114 us  [on_device(): pl.pallas_call(functools.partial(sublayer, sections, experts, tensors), o...]
    unnamed x3 -> x1, local copies, waits for them, and re-layouts: 4.45 us -> 1.97 us
where the time goes in v2:
time: 116 us
  Pallas kernels  114 us (98%)
  local copies, waits for them, and re-layouts  1.97 us (2%)
    pallas_call x1, Pallas kernels, on_device(): pl.pallas_call(functools.partial(sublayer, sections, experts, tensors), o...  114 us

profile of v2, /device:TPU:0, one launch (start us, length us, event | category | flops | bytes accessed | tf_op | source)
XLA Modules:
  0.0 116.2 jit_solution(15211430618968071358)
XLA Ops:
  0.0 114.2 %shard_map.73 = bf16[128,2560]{1,0:T(8,128)(2,1)} custom-call(bf16[128,2560]{1,0:T(8,128)(2,1)} %tokens_ref.1, f32[2560]{0:T(1024)} %gain_ref.1, bf16[4,2560]{1,0:T(4,128)(2,1)} %bitcast.2, s32[1,128]{1,0:T(1,128)} %bitcast.3, bf16[1,5120,512]{2,1,0:T(8,128)(2,1)} %gate_hbm.1, bf16[1,5120,512]{2,1,0:T(8,128)(2,1)} %up_hbm.1, bf16[1,1024,2560]{2,1,0:T(8,128)(2,1)} %down_hbm.1), custom_call_target="tpu_custom_call" | custom-call | tf_op jit(solution)/shard_map/pallas_call | solution.py:414
  114.2 2.0 %copy.9 = bf16[128,2560]{1,0:T(8,128)(2,1)} copy(bf16[128,2560]{1,0:T(8,128)(2,1)} %shard_map.73) | data formatting | bytes 1310720

commit v3 on v2

--- a/solution.py
+++ b/solution.py
@@ -15,7 +15,7 @@
 
 
 def tile_of(width):
-    for tile in (512, 256, 128):
+    for tile in (1280, 640, 512, 256, 128):
         if width % tile == 0:
             return tile
     return width

time: 116 us -> 112 us (0.966)
  Pallas kernels: 114 us -> 110 us
    pallas_call x1, Pallas kernels: 114 us -> 110 us  [on_device(): pl.pallas_call(functools.partial(sublayer, sections, experts, tensors), o...]
where the time goes in v3:
time: 112 us
  Pallas kernels  110 us (98%)
  local copies, waits for them, and re-layouts  1.97 us (2%)
    pallas_call x1, Pallas kernels, on_device(): pl.pallas_call(functools.partial(sublayer, sections, experts, tensors), o...  110 us

profile of v3, /device:TPU:0, one launch (start us, length us, event | category | flops | bytes accessed | tf_op | source)
XLA Modules:
  0.0 111.5 jit_solution(17282307642464985880)
XLA Ops:
  0.0 109.5 %shard_map.73 = bf16[128,2560]{1,0:T(8,128)(2,1)} custom-call(bf16[128,2560]{1,0:T(8,128)(2,1)} %tokens_ref.1, f32[2560]{0:T(1024)} %gain_ref.1, bf16[4,2560]{1,0:T(4,128)(2,1)} %bitcast.2, s32[1,128]{1,0:T(1,128)} %bitcast.3, bf16[1,5120,512]{2,1,0:T(8,128)(2,1)} %gate_hbm.1, bf16[1,5120,512]{2,1,0:T(8,128)(2,1)} %up_hbm.1, bf16[1,1024,2560]{2,1,0:T(8,128)(2,1)} %down_hbm.1), custom_call_target="tpu_custom_call" | custom-call | tf_op jit(solution)/shard_map/pallas_call | solution.py:414
  109.5 2.0 %copy.9 = bf16[128,2560]{1,0:T(8,128)(2,1)} copy(bf16[128,2560]{1,0:T(8,128)(2,1)} %shard_map.73) | data formatting | bytes 1310720
